TPU v7x, 32 devices: a whole 2x2x4 slice. The times are simulated.
32 devices in a mesh: grp: 2 (over y), ek: 8 (over z, x), per: 2 (over core).
Axes of the slice: x: 2, y: 2, z: 4, core: 2. Of those that a mesh axis runs over, the one named last changes fastest.
Arguments:
- retarded: bfloat16 [2, 32, 2, 640, 640], P('per', ('grp', 'ek')), parts along dimension 1, may hold values from -0.25 to 0.25
- scatter_root: float32 [2, 32, 640], P('per', ('grp', 'ek')), parts along dimension 1, may hold values from 0.2 to 1
- coupling: bfloat16 [640, 640], replicated, may hold values from -0.15625 to 0.15625
- source_index: int32 [16, 16], replicated, may hold values from 0 to 15
- kernel_weight: float32 [16, 16], replicated, may hold values from 0.02 to 0.5
Outputs:
- sigma_less: bfloat16 [2, 32, 2, 640, 640], P('per', 'grp', None, 'ek'), parts along dimension 1
There are 2 independent parts, one for each index of `grp`. A program takes and returns all parts, laid end to end along the dimension named above; an argument that names none is the same for every part. Nothing has to cross between parts.
Inputs may be any that keep to these rules, and one draw needn't show every extreme that they name: `source_index`: source energy-k points of the phonon and roughness kernel.
All inputs are finite; a program needn't handle non-finite values.
Results may differ from a plain program's by a relative error of at most 0.0055.
Values may be sent and summed in bfloat16 or wider, within the bound.
A program may use at most 64 MiB of HBM per device.

v0:
```python
import functools
import jax
import jax.numpy as jnp
from jax import lax
from jax.experimental import pallas as pl
from jax.experimental.pallas import tpu as pltpu
from jax.sharding import PartitionSpec as P


def shifted(array, axis, by):
    size = lax.axis_size(axis)
    pairs = [(i, i + by) for i in range(size) if 0 <= i + by < size]
    return lax.ppermute(array, axis, pairs)


def product(former, latter):
    return jnp.dot(former, latter, preferred_element_type=jnp.float32)


def transposed_product(former, latter):
    return lax.dot_general(
        former, latter, (((1,), (1,)), ((), ())), preferred_element_type=jnp.float32
    )


def build_kernel(source_index, kernel_weight, total_points):
    targets = jnp.arange(total_points, dtype=jnp.int32)
    matches = (source_index[:, :, None] == targets[None, None, :]).astype(jnp.float32)
    return jnp.sum(kernel_weight[:, :, None] * matches, axis=1).astype(jnp.bfloat16)


def local_parts(real_g, imag_g, amplitude):
    root_real = (real_g * amplitude[None, :]).astype(jnp.bfloat16)
    root_imag = (imag_g * amplitude[None, :]).astype(jnp.bfloat16)
    local_real = transposed_product(root_real, root_real) + transposed_product(root_imag, root_imag)
    skewed = transposed_product(root_imag, root_real)
    return (local_real, skewed - skewed.T)


def coupled_parts(real_g, imag_g, coupling):
    return (
        product(real_g, coupling).astype(jnp.bfloat16),
        product(imag_g, coupling).astype(jnp.bfloat16),
    )


def advance(local_pair, coupled_pair, carried_in):
    coupled_real, coupled_imag = coupled_pair
    prev_real = carried_in[0]
    prev_imag = carried_in[1]
    carried_real = (product(coupled_real, prev_real) - product(coupled_imag, prev_imag)).astype(
        jnp.bfloat16
    )
    carried_imag = (product(coupled_real, prev_imag) + product(coupled_imag, prev_real)).astype(
        jnp.bfloat16
    )
    new_real = (
        local_pair[0]
        + transposed_product(carried_real, coupled_real)
        + transposed_product(carried_imag, coupled_imag)
    )
    new_imag = (
        local_pair[1]
        + transposed_product(carried_imag, coupled_real)
        - transposed_product(carried_real, coupled_imag)
    )
    return jnp.stack([new_real.astype(jnp.bfloat16), new_imag.astype(jnp.bfloat16)])


def body(retarded, scatter_root, coupling, source_index, kernel_weight):
    points_dev = retarded.shape[1]
    states = retarded.shape[3]
    groups = lax.axis_size("ek")
    total_points = points_dev * groups
    row_count = states // groups
    kernel = build_kernel(source_index, kernel_weight, total_points)
    local_terms = []
    coupled_terms = []
    lesser = []
    for member in range(points_dev):
        real_g = retarded[0, member, 0]
        imag_g = retarded[0, member, 1]
        local_pair = local_parts(real_g, imag_g, scatter_root[0, member])
        local_terms.append(local_pair)
        coupled_terms.append(coupled_parts(real_g, imag_g, coupling))
        lesser.append(
            jnp.stack([local_pair[0].astype(jnp.bfloat16), local_pair[1].astype(jnp.bfloat16)])
        )
    carried = shifted(jnp.stack(lesser), "per", 1)
    lesser = [
        advance(local_terms[member], coupled_terms[member], carried[member])
        for member in range(points_dev)
    ]
    stacked = jnp.stack(lesser)[None]
    regrouped = lax.all_to_all(stacked, "ek", split_axis=3, concat_axis=1, tiled=True)
    summed = product(kernel, regrouped.reshape(total_points, -1))
    return summed.astype(jnp.bfloat16).reshape(1, total_points, 2, row_count, states)


SUB = 16
LIMIT = 48
MESH = pl.DeviceIdType.MESH


def fused(
    groups,
    retarded,
    scatter,
    coupling_ref,
    index_ref,
    weight_ref,
    out,
    green,
    coupling,
    stack,
    pair,
    moved,
    local,
    lesser,
    before,
    received,
    result,
    spread,
    load_sem,
    coupling_sem,
    self_sem,
    send_sem,
    recv_sem,
    hand_sem,
    take_sem,
    out_sem,
):
    me = lax.axis_index("ek")
    period = lax.axis_index("per")
    points = green.shape[0]
    states = green.shape[2]
    rows = states // groups
    half = groups // 2
    total = points * groups
    tile = states // 2

    def load(member, part):
        return pltpu.make_async_copy(
            retarded.at[0, member, part], green.at[member, part], load_sem.at[member, part]
        )

    for member in range(points):
        for part in range(2):
            load(member, part).start()
    fetch = pltpu.make_async_copy(coupling_ref, coupling, coupling_sem)
    fetch.start()

    barrier = pltpu.get_barrier_semaphore()
    for step in range(1, groups):
        pl.semaphore_signal(
            barrier, inc=1, device_id={"ek": (me + step) % groups}, device_id_type=MESH
        )
    pl.semaphore_signal(barrier, inc=1, device_id={"per": 1 - period}, device_id_type=MESH)

    upper = me // half
    place = me % half

    def band(target):
        return pl.ds(pl.multiple_of(target * rows, SUB), rows)

    def send(member, part, slot, target):
        return pltpu.make_async_remote_copy(
            src_ref=lesser.at[member, part, band(target), :],
            dst_ref=received.at[me * points + member, part],
            send_sem=send_sem.at[member, part, slot],
            recv_sem=recv_sem.at[me * points + member, part],
            device_id={"ek": target},
            device_id_type=MESH,
        )

    def keep(member, part):
        return pltpu.make_async_copy(
            lesser.at[member, part, band(me), :],
            received.at[me * points + member, part],
            self_sem.at[member, part],
        )

    def hand(member):
        return pltpu.make_async_remote_copy(
            src_ref=lesser.at[member],
            dst_ref=before.at[member],
            send_sem=hand_sem.at[member],
            recv_sem=take_sem.at[member],
            device_id={"per": 1 - period},
            device_id_type=MESH,
        )

    def send_tile(member, part, at):
        for step in range(half):
            target = at * half + (place + step) % half

            @pl.when(target != me)
            def _():
                send(member, part, target, target).start()

            @pl.when(target == me)
            def _():
                keep(member, part).start()

    def tiles(body, first, after=None):
        for part in range(2):

            @pl.loop(0, 2)
            def _(step):
                at = (first + step) % 2
                start = at * tile
                body(
                    part,
                    pl.ds(pl.multiple_of(start, SUB), tile),
                    pl.ds(pl.multiple_of(part * states + start, SUB), tile),
                )
                if after is not None:
                    after(part, at)

    def find_local(member, first):
        for part in range(2):
            load(member, part).wait()
        scale = scatter[0, pl.ds(member, 1), :]
        real = (green[member, 0].astype(jnp.float32) * scale).astype(jnp.bfloat16)
        imag = (green[member, 1].astype(jnp.float32) * scale).astype(jnp.bfloat16)
        stack[:states, :states] = real
        stack[states:, states:] = -real
        stack[:states, states:] = imag
        stack[states:, :states] = imag

        def one(part, rows_at, stacked_at):
            value = transposed_product(stack[stacked_at, :], stack[:states, :])
            local[member, part, rows_at, :] = value
            lesser[member, part, rows_at, :] = value.astype(jnp.bfloat16)

        def leave(part, at):
            @pl.when(period == 0)
            def _():
                send_tile(member, part, at)

        tiles(one, first, leave)

    def find_coupled(member):
        def one(part, rows_at, stacked_at):
            value = product(green[member, part, rows_at, :], coupling[...]).astype(jnp.bfloat16)
            if part == 0:
                pair[member, rows_at, :states] = value
                pair[member, pl.ds(stacked_at.start + states, tile), states:] = value
            else:
                pair[member, pl.ds(stacked_at.start - states, tile), states:] = -value
                pair[member, stacked_at, :states] = value

        tiles(one, 0)

    def advance_point(member):
        def carry(part, rows_at, stacked_at):
            value = (
                product(pair[member, stacked_at, :states], before[member, 0])
                + product(pair[member, stacked_at, states:], before[member, 1])
            ).astype(jnp.bfloat16)
            if part == 0:
                moved[rows_at, states:] = value
                moved[pl.ds(stacked_at.start + states, tile), :states] = -value
            else:
                moved[rows_at, :states] = value
                moved[stacked_at, states:] = value

        tiles(carry, 0)

        def close(part, rows_at, stacked_at):
            value = local[member, part, rows_at, :] + transposed_product(
                moved[stacked_at, :], pair[member, states:, :]
            )
            lesser[member, part, rows_at, :] = value.astype(jnp.bfloat16)

        tiles(close, upper, functools.partial(send_tile, member))

    fetch.wait()
    pl.semaphore_wait(barrier, groups)

    def give(member):
        @pl.when(period == 0)
        def _():
            hand(member).start()

    find_local(0, 1 - upper)
    give(0)

    @pl.loop(1, points)
    def _(member):
        find_local(member, upper)
        give(member)

    @pl.when(period == 1)
    def _():
        @pl.loop(0, points)
        def _(member):
            find_coupled(member)
            hand(member).wait_recv()
            advance_point(member)

    source = index_ref[...]
    weight = weight_ref[...]
    column = lax.broadcasted_iota(jnp.int32, (total, total), 1)
    matrix = jnp.zeros((total, total), jnp.float32)
    for tap in range(source.shape[1]):
        matrix = matrix + jnp.where(
            source[:, tap : tap + 1] == column, weight[:, tap : tap + 1], 0.0
        )
    matrix = matrix.astype(jnp.bfloat16)
    long = total * SUB
    expand = jnp.where(
        lax.broadcasted_iota(jnp.int32, (long, total), 0) // SUB
        == lax.broadcasted_iota(jnp.int32, (long, total), 1),
        1.0,
        0.0,
    ).astype(jnp.bfloat16)
    wide = transposed_product(product(expand, matrix).astype(jnp.bfloat16), expand)
    same = (
        lax.broadcasted_iota(jnp.int32, (long, long), 0) % SUB
        == lax.broadcasted_iota(jnp.int32, (long, long), 1) % SUB
    )
    spread[...] = jnp.where(same, wide, 0.0).astype(jnp.bfloat16)

    def store(part):
        return pltpu.make_async_copy(result.at[part], out.at[0, :, part], out_sem.at[part])

    @pl.loop(0, points)
    def _(member):
        for part in range(2):
            keep(member, part).wait()

    for part in range(2):

        @pl.loop(1, groups)
        def _(step):
            other = (me + step) % groups

            @pl.loop(0, points)
            def _(member):
                pltpu.make_async_remote_copy(
                    src_ref=lesser.at[member, part, band(other), :],
                    dst_ref=received.at[other * points + member, part],
                    send_sem=send_sem.at[member, part, 0],
                    recv_sem=recv_sem.at[other * points + member, part],
                    device_id={"ek": other},
                    device_id_type=MESH,
                ).wait_recv()

        @pl.loop(0, rows // SUB)
        def _(at):
            span = pl.ds(pl.multiple_of(at * SUB, SUB), SUB)
            value = product(spread[...], received[:, part, span, :].reshape(long, states))
            result[part, :, span, :] = value.astype(jnp.bfloat16).reshape(total, SUB, states)

        store(part).start()

    @pl.loop(0, points)
    def _(member):
        for part in range(2):
            for step in range(1, groups):
                target = (me + step) % groups
                send(member, part, target, target).wait_send()

        @pl.when(period == 0)
        def _():
            hand(member).wait_send()

    for part in range(2):
        store(part).wait()


def fused_body(groups, retarded, scatter_root, coupling, source_index, kernel_weight):
    points = retarded.shape[1]
    states = retarded.shape[3]
    rows = states // groups
    total = points * groups
    dma = pltpu.SemaphoreType.DMA
    wide = jnp.bfloat16
    whole = pl.BlockSpec(memory_space=pltpu.VMEM)
    return pl.pallas_call(
        functools.partial(fused, groups),
        out_shape=jax.ShapeDtypeStruct((1, total, 2, rows, states), wide),
        in_specs=[
            pl.BlockSpec(memory_space=pl.ANY),
            whole,
            pl.BlockSpec(memory_space=pl.ANY),
            whole,
            whole,
        ],
        out_specs=pl.BlockSpec(memory_space=pl.ANY),
        scratch_shapes=[
            pltpu.VMEM((points, 2, states, states), wide),
            pltpu.VMEM((states, states), wide),
            pltpu.VMEM((2 * states, 2 * states), wide),
            pltpu.VMEM((points, 2 * states, 2 * states), wide),
            pltpu.VMEM((2 * states, 2 * states), wide),
            pltpu.VMEM((points, 2, states, states), jnp.float32),
            pltpu.VMEM((points, 2, states, states), wide),
            pltpu.VMEM((points, 2, states, states), wide),
            pltpu.VMEM((total, 2, rows, states), wide),
            pltpu.VMEM((2, total, rows, states), wide),
            pltpu.VMEM((total * SUB, total * SUB), wide),
            dma((points, 2)),
            dma,
            dma((points, 2)),
            dma((points, 2, groups)),
            dma((total, 2)),
            dma((points,)),
            dma((points,)),
            dma((2,)),
        ],
        compiler_params=pltpu.CompilerParams(
            collective_id=0, has_side_effects=True, vmem_limit_bytes=LIMIT * 1024 * 1024
        ),
    )(retarded, scatter_root, coupling, source_index, kernel_weight)


def solution(mesh):
    groups = mesh.shape["ek"]

    def chosen(retarded, *others):
        states = retarded.shape[3]
        fits = states % (groups * SUB) == 0 and mesh.shape["per"] == 2 and groups % 2 == 0
        if fits:
            return fused_body(groups, retarded, *others)
        return body(retarded, *others)

    in_specs = (
        P("per", ("grp", "ek"), None, None, None),
        P("per", ("grp", "ek"), None),
        P(),
        P(),
        P(),
    )
    out_specs = P("per", "grp", None, "ek", None)
    return jax.shard_map(chosen, mesh=mesh, in_specs=in_specs, out_specs=out_specs, check_vma=False)
```

profile of v0, /device:TPU:1, one launch (start us, length us, event | category | flops | bytes accessed | tf_op | source)
XLA Modules:
  0.0 86.6 jit_solution(14735733701483908593)
XLA Ops:
  0.0 0.0 copy-start
  0.0 1.1 %copy-done = bf16[640,640]{1,0:T(8,128)(2,1)S(1)} copy-done((bf16[640,640]{1,0:T(8,128)(2,1)S(1)}, bf16[640,640]{1,0:T(8,128)(2,1)}, u32[]{:S(2)}) %copy-start) | copy-done | bytes 819224
  1.1 0.0 copy-start.1
  1.1 0.7 copy-done.1
  1.8 0.0 copy-start.2
  1.8 0.7 copy-done.2
  2.5 0.0 copy-start.3
  2.5 0.7 copy-done.3
  3.2 81.7 %shard_map.55 = bf16[1,16,2,80,640]{4,3,2,1,0:T(8,128)(2,1)S(1)} custom-call(bf16[1,2,2,640,640]{4,3,2,1,0:T(8,128)(2,1)} %retarded.1, f32[1,2,640]{2,1,0:T(2,128)S(1)} %copy-done.3, bf16[640,640]{1,0:T(8,128)(2,1)S(1)} %copy-done, s32[16,16]{1,0:T(8,128)S(1)} %copy-done.1, f32[16,16]{1,0:T(8,128)S(1)} %copy-done.2), custom_call_target="tpu_custom_call" | custom-call | tf_op jit(solution)/shard_map/pallas_call | solution.py:381
  84.9 1.7 %copy.7 = bf16[1,16,2,80,640]{4,3,2,1,0:T(8,128)(2,1)} copy(bf16[1,16,2,80,640]{4,3,2,1,0:T(8,128)(2,1)S(1)} %shard_map.55) | data formatting | bytes 6553600
Async XLA Ops:
  0.0 1.1 %copy-start = (bf16[640,640]{1,0:T(8,128)(2,1)S(1)}, bf16[640,640]{1,0:T(8,128)(2,1)}, u32[]{:S(2)}) copy-start(bf16[640,640]{1,0:T(8,128)(2,1)} %coupling_ref.1) | copy-start | bytes 2457604
  1.1 0.7 copy-start.1
  1.8 0.7 copy-start.2
  2.5 0.7 copy-start.3
where the time goes:
time: 86.9 us; the launch traced here: 86.6 us
  Pallas kernels  81.7 us (94%)
  local copies, waits for them, and re-layouts  4.94 us (6%)
    pallas_call x1, Pallas kernels, fused_body(): pl.pallas_call(functools.partial(fused, groups), out_shape=jax.ShapeDtype...  81.7 us
    unnamed x9, local copies, waits for them, and re-layouts  4.94 us

commit v1 on v0

v1 whole, which is shorter than its diff:
```python
import jax
import jax.numpy as jnp
from jax import lax
from jax.experimental import pallas as pl
from jax.experimental.pallas import tpu as pltpu
from jax.sharding import PartitionSpec as P


def shifted(array, axis, by):
    size = lax.axis_size(axis)
    pairs = [(i, i + by) for i in range(size) if 0 <= i + by < size]
    return lax.ppermute(array, axis, pairs)


def product(former, latter):
    return jnp.dot(former, latter, preferred_element_type=jnp.float32)


def transposed_product(former, latter):
    return lax.dot_general(
        former, latter, (((1,), (1,)), ((), ())), preferred_element_type=jnp.float32
    )


def build_kernel(source_index, kernel_weight, total_points):
    targets = jnp.arange(total_points, dtype=jnp.int32)
    matches = (source_index[:, :, None] == targets[None, None, :]).astype(jnp.float32)
    return jnp.sum(kernel_weight[:, :, None] * matches, axis=1).astype(jnp.bfloat16)


def local_parts(real_g, imag_g, amplitude):
    root_real = (real_g * amplitude[None, :]).astype(jnp.bfloat16)
    root_imag = (imag_g * amplitude[None, :]).astype(jnp.bfloat16)
    local_real = transposed_product(root_real, root_real) + transposed_product(root_imag, root_imag)
    skewed = transposed_product(root_imag, root_real)
    return (local_real, skewed - skewed.T)


def coupled_parts(real_g, imag_g, coupling):
    return (
        product(real_g, coupling).astype(jnp.bfloat16),
        product(imag_g, coupling).astype(jnp.bfloat16),
    )


def advance(local_pair, coupled_pair, carried_in):
    coupled_real, coupled_imag = coupled_pair
    prev_real = carried_in[0]
    prev_imag = carried_in[1]
    carried_real = (product(coupled_real, prev_real) - product(coupled_imag, prev_imag)).astype(
        jnp.bfloat16
    )
    carried_imag = (product(coupled_real, prev_imag) + product(coupled_imag, prev_real)).astype(
        jnp.bfloat16
    )
    new_real = (
        local_pair[0]
        + transposed_product(carried_real, coupled_real)
        + transposed_product(carried_imag, coupled_imag)
    )
    new_imag = (
        local_pair[1]
        + transposed_product(carried_imag, coupled_real)
        - transposed_product(carried_real, coupled_imag)
    )
    return jnp.stack([new_real.astype(jnp.bfloat16), new_imag.astype(jnp.bfloat16)])


def body(retarded, scatter_root, coupling, source_index, kernel_weight):
    points_dev = retarded.shape[1]
    states = retarded.shape[3]
    groups = lax.axis_size("ek")
    total_points = points_dev * groups
    row_count = states // groups
    kernel = build_kernel(source_index, kernel_weight, total_points)
    local_terms = []
    coupled_terms = []
    lesser = []
    for member in range(points_dev):
        real_g = retarded[0, member, 0]
        imag_g = retarded[0, member, 1]
        local_pair = local_parts(real_g, imag_g, scatter_root[0, member])
        local_terms.append(local_pair)
        coupled_terms.append(coupled_parts(real_g, imag_g, coupling))
        lesser.append(
            jnp.stack([local_pair[0].astype(jnp.bfloat16), local_pair[1].astype(jnp.bfloat16)])
        )
    carried = shifted(jnp.stack(lesser), "per", 1)
    lesser = [
        advance(local_terms[member], coupled_terms[member], carried[member])
        for member in range(points_dev)
    ]
    stacked = jnp.stack(lesser)[None]
    regrouped = lax.all_to_all(stacked, "ek", split_axis=3, concat_axis=1, tiled=True)
    summed = product(kernel, regrouped.reshape(total_points, -1))
    return summed.astype(jnp.bfloat16).reshape(1, total_points, 2, row_count, states)


SUB = 16
LIMIT = 58
MESH = pl.DeviceIdType.MESH


def fused(
    retarded,
    scatter_ref,
    coupling_ref,
    index_ref,
    weight_ref,
    out,
    green,
    scatter,
    coupling,
    index,
    weight,
    stack,
    pair,
    moved,
    total,
    blocks,
    before,
    cross,
    diag,
    got_x,
    got_c,
    got_d,
    got_o,
    res_c,
    res_d,
    inner,
    result,
    spread,
    spread_d,
    load_sem,
    small_sem,
    keep_x,
    keep_c,
    keep_d,
    x_send,
    x_recv,
    c_send,
    c_side,
    c_on,
    c_recv,
    d_send,
    d_side,
    d_recv,
    o_send,
    o_on,
    o_recv,
    hand_sem,
    take_sem,
    out_sem,
):
    groups, points = got_x.shape[:2]
    me = lax.axis_index("ek")
    period = lax.axis_index("per")
    states = green.shape[2]
    wide = states // 2
    level = states // 4
    rows = states // groups
    count = points * groups

    half = me // 4
    place = me // 2
    side = me % 2
    low = place % 2
    far = 1 - half
    entry = 1 + half
    other = 4 * half + 1 - place
    beside = 2 * place + 1 - side
    across = 2 * other + side
    far_near = 2 * (2 - half) + side
    far_end = 2 * (3 * far) + side
    at_entry = place == entry

    def load(point, part):
        return pltpu.make_async_copy(
            retarded.at[0, point, part], green.at[point, part], load_sem.at[point, part]
        )

    small = [
        pltpu.make_async_copy(scatter_ref, scatter, small_sem.at[0]),
        pltpu.make_async_copy(coupling_ref, coupling, small_sem.at[1]),
        pltpu.make_async_copy(index_ref, index, small_sem.at[2]),
        pltpu.make_async_copy(weight_ref, weight, small_sem.at[3]),
    ]
    small[0].start()
    for part in range(2):
        load(0, part).start()
    small[1].start()
    for part in range(2):
        load(1, part).start()
    small[2].start()
    small[3].start()

    barrier = pltpu.get_barrier_semaphore()
    for step in range(1, groups):
        pl.semaphore_signal(
            barrier, inc=1, device_id={"ek": (me + step) % groups}, device_id_type=MESH
        )
    pl.semaphore_signal(barrier, inc=1, device_id={"per": 1 - period}, device_id_type=MESH)

    def span(start, size):
        return pl.ds(pl.multiple_of(start, SUB), size)

    def remote(source, target, sent, landed, device):
        return pltpu.make_async_remote_copy(
            src_ref=source,
            dst_ref=target,
            send_sem=sent,
            recv_sem=landed,
            device_id={"ek": device},
            device_id_type=MESH,
        )

    def send_x(point, device):
        return remote(
            blocks.at[point, 1 - device // 4, span(device * rows, rows), :],
            got_x.at[me, point],
            x_send.at[device, point],
            x_recv.at[me, point],
            device,
        )

    def wait_x(point, device):
        remote(
            got_x.at[device, point],
            got_x.at[device, point],
            x_send.at[device, point],
            x_recv.at[device, point],
            device,
        ).wait_recv()

    def send_c(point, which, slot, device):
        return remote(
            cross.at[which, point],
            got_c.at[me, point],
            c_send.at[slot, point],
            c_recv.at[me, point],
            device,
        )

    def side_c(point, source):
        here = got_c.at[source, point]
        return remote(here, here, c_side.at[source, point], c_recv.at[source, point], beside)

    def on_c(point, source, slot):
        here = got_c.at[source, point]
        return remote(here, here, c_on.at[slot, point], c_recv.at[source, point], across)

    def send_d(which, bit, slot, device):
        return remote(
            diag.at[which, bit], got_d.at[me], d_send.at[slot], d_recv.at[me], device
        )

    def side_d(source):
        here = got_d.at[source]
        return remote(here, here, d_side.at[source], d_recv.at[source], beside)

    def send_o():
        slot = jnp.where(at_entry, 0, 1)
        return remote(
            diag.at[far, far], got_o.at[slot], o_send, o_recv.at[slot], far_near
        )

    def wait_o(slot, source):
        remote(
            got_o.at[slot], got_o.at[slot], o_on.at[slot], o_recv.at[slot], source
        ).wait_recv()

    def on_o(slot, source):
        return remote(
            got_o.at[slot], got_d.at[source], o_on.at[slot], d_recv.at[source], across
        )

    def hand(point):
        return pltpu.make_async_remote_copy(
            src_ref=blocks.at[point],
            dst_ref=before.at[point],
            send_sem=hand_sem.at[point],
            recv_sem=take_sem.at[point],
            device_id={"per": 1 - period},
            device_id_type=MESH,
        )

    def own_x(point):
        return pltpu.make_async_copy(
            blocks.at[point, far, span(me * rows, rows), :], got_x.at[me, point], keep_x.at[point]
        )

    def own_c(point):
        return pltpu.make_async_copy(
            cross.at[half, point], got_c.at[me, point], keep_c.at[point]
        )

    def own_d():
        return pltpu.make_async_copy(diag.at[half, low], got_d.at[me], keep_d)

    def fill_stack(point):
        for part in range(2):
            load(point, part).wait()
        scale = scatter[0, pl.ds(point, 1), :]
        for band in range(2):
            at = slice(band * wide, (band + 1) * wide)
            real = (green[point, 0, at, :].astype(jnp.float32) * scale).astype(jnp.bfloat16)
            imag = (green[point, 1, at, :].astype(jnp.float32) * scale).astype(jnp.bfloat16)
            top = slice(band * states, band * states + wide)
            low_at = slice(band * states + wide, (band + 1) * states)
            stack[top, :states] = real
            stack[top, states:] = imag
            stack[low_at, :states] = -imag
            stack[low_at, states:] = real

    def fill_pair(point):
        @pl.loop(0, 2)
        def _(band):
            at = span(band * wide, wide)
            real = product(green[point, 0, at, :], coupling[...]).astype(jnp.bfloat16)
            imag = product(green[point, 1, at, :], coupling[...]).astype(jnp.bfloat16)
            top = span(band * states, wide)
            low_at = span(band * states + wide, wide)
            pair[top, :states] = real
            pair[top, states:] = imag
            pair[low_at, :states] = -imag
            pair[low_at, states:] = real

    def fill_moved(point):
        @pl.loop(0, 2)
        def _(band):
            at = span(band * wide, wide)
            top = span(band * states, wide)
            for part in range(2):
                straight = product(pair[top, :states], before[point, part])
                turned = product(pair[top, states:], before[point, part])
                real = straight[:, :wide] - turned[:, wide:]
                imag = straight[:, wide:] + turned[:, :wide]
                moved[at, part * wide : (part + 1) * wide] = real.astype(jnp.bfloat16)
                moved[at, states + part * wide : states + (part + 1) * wide] = imag.astype(
                    jnp.bfloat16
                )

    def block(upper, lower):
        total[...] = transposed_product(
            stack[span(upper * states, wide), :], stack[span(lower * states, states), :]
        )

        @pl.when(period == 1)
        def _():
            total[...] += transposed_product(
                moved[span(upper * wide, wide), :], pair[span(lower * states, states), :]
            )

    row = lax.broadcasted_iota(jnp.int32, (level, level), 0)
    column = lax.broadcasted_iota(jnp.int32, (level, level), 1)
    upper_part = row <= column

    def folded(value):
        return [value[:rows, :], value[rows:, :]]

    def diagonal(point, which):
        block(which, which)
        blocks[point, which, span(which * wide, wide), :] = total[...].astype(jnp.bfloat16)
        real = total[:level, level : 2 * level]
        imag = total[:level, 3 * level :]
        cross[which, point] = jnp.concatenate(folded(real) + folded(imag), axis=1).astype(
            jnp.bfloat16
        )
        for bit in range(2):
            at = slice(bit * level, (bit + 1) * level)
            packed = jnp.where(
                upper_part,
                total[at, bit * level : (bit + 1) * level],
                total[at, (2 + bit) * level : (3 + bit) * level],
            )
            kept = jnp.concatenate(folded(packed), axis=1).astype(jnp.bfloat16)
            for member in range(points):

                @pl.when(point == member)
                def _():
                    diag[which, bit, :, member * wide : (member + 1) * wide] = kept

    def crossing(point, which):
        block(which, 1 - which)
        blocks[point, 1 - which, span(which * wide, wide), :] = total[...].astype(jnp.bfloat16)

    @pl.loop(0, points)
    def _(point):
        @pl.when(point == 0)
        def _():
            small[0].wait()

        fill_stack(point)

        @pl.when(period == 1)
        def _():
            @pl.when(point == 0)
            def _():
                small[1].wait()

            fill_pair(point)

            @pl.when(point == 0)
            def _():
                pl.semaphore_wait(barrier, groups)

            hand(point).wait_recv()
            fill_moved(point)

        @pl.loop(0, 2)
        def _(step):
            which = jnp.where(step == 0, far, half)
            diagonal(point, which)

            @pl.when((period == 0) & (point == 0) & (step == 0))
            def _():
                pl.semaphore_wait(barrier, groups)

            @pl.when(step == 0)
            def _():
                send_c(point, far, 0, far_near).start()

                @pl.when(point == points - 1)
                def _():
                    send_o().start()
                    send_d(far, 1 - far, 0, far_near).start()

            @pl.when(step == 1)
            def _():
                send_c(point, half, 1, beside).start()
                send_c(point, half, 2, across).start()
                own_c(point).start()

                @pl.when(point == points - 1)
                def _():
                    send_d(half, low, 1, beside).start()
                    send_d(half, 1 - low, 2, across).start()
                    own_d().start()

            crossing(point, which)

            @pl.when(step == 0)
            def _():
                for device in (
                    4 * far + 2 * far + 1 - side,
                    4 * far + 2 * half + 1 - side,
                    4 * far + 2 * far + side,
                    4 * far + 2 * half + side,
                ):
                    send_x(point, device).start()

            @pl.when(step == 1)
            def _():
                for device in (2 * other + 1 - side, across, beside):
                    send_x(point, device).start()
                own_x(point).start()

        @pl.when(period == 0)
        def _():
            hand(point).start()

    @pl.when(period == 0)
    def _():
        small[1].wait()

    def pass_c(point, source, slot):
        side_c(point, source).wait_recv()
        if slot is not None:

            @pl.when(at_entry)
            def _():
                on_c(point, source, slot).start()

        side_c(point, source).start()

    def pass_d(source, slot):
        if slot is not None:

            @pl.when(at_entry)
            def _():
                wait_o(slot, source)
                on_o(slot, source).start()

        side_d(source).wait_recv()
        side_d(source).start()

    passing = ((far_near, 0), (across, None), (far_end, 1))
    for point in range(points):
        for source, slot in passing:
            pass_c(point, source, slot)
    for source, slot in passing:
        pass_d(source, slot)

    small[2].wait()
    small[3].wait()
    long = count * SUB
    source_of = index[...]
    value_of = weight[...]
    target = lax.broadcasted_iota(jnp.int32, (count, count), 1)
    matrix = jnp.zeros((count, count), jnp.float32)
    for tap in range(index.shape[1]):
        matrix = matrix + jnp.where(
            source_of[:, tap : tap + 1] == target, value_of[:, tap : tap + 1], 0.0
        )
    matrix = matrix.astype(jnp.bfloat16)

    def ones(mask):
        return jnp.where(mask, 1.0, 0.0).astype(jnp.bfloat16)

    def iota(shape, axis):
        return lax.broadcasted_iota(jnp.int32, shape, axis)

    tall = ones(iota((long, count), 0) // SUB == iota((long, count), 1))
    grown = product(tall, matrix).astype(jnp.bfloat16)
    spread[...] = jnp.where(
        iota((long, long), 0) % SUB == iota((long, long), 1) % SUB,
        transposed_product(grown, tall),
        0.0,
    ).astype(jnp.bfloat16)
    short = groups * SUB
    for member in range(points):
        picked = ones(
            (iota((short, count), 0) // SUB) * points + member == iota((short, count), 1)
        )
        spread_d[member] = jnp.where(
            iota((long, short), 0) % SUB == iota((long, short), 1) % SUB,
            transposed_product(grown, picked),
            0.0,
        ).astype(jnp.bfloat16)

    own_d().wait()
    for point in range(points):
        own_c(point).wait()
    for stage in range(groups // 2):
        source = 2 * stage + 1 - side
        for point in range(points):
            side_c(point, source).wait_recv()
        side_d(source).wait_recv()

    @pl.loop(0, rows // SUB)
    def _(at):
        here = span(at * SUB, SUB)
        after = span(rows + at * SUB, SUB)
        value = product(spread[...], got_c[:, :, here, :].reshape(long, states))
        res_c[:, here, :] = value.astype(jnp.bfloat16).reshape(count, SUB, states)
        value = pltpu.roll(value, states - level, 1)
        res_c[:, after, :] = value.astype(jnp.bfloat16).reshape(count, SUB, states)
        taken = got_d[:, here, :].reshape(short, states)
        value = (
            product(spread_d[0], taken)[:, :wide] + product(spread_d[1], taken)[:, wide:]
        )
        first = value[:, :level].astype(jnp.bfloat16)
        second = value[:, level:].astype(jnp.bfloat16)
        res_d[:, here, :] = first.reshape(count, SUB, level)
        res_d[:, after, :] = second.reshape(count, SUB, level)

    row_at = iota((rows, level), 0) + side * rows
    column_at = iota((rows, level), 1)
    pick = ones(row_at == column_at)
    outer = low == 0

    @pl.loop(0, count)
    def _(t):
        mine = span(side * rows, rows)
        straight = res_d[t, mine, :].astype(jnp.float32)
        turned = transposed_product(pick, res_d[t])
        own_real = jnp.where(column_at >= row_at, straight, turned)
        own_imag = jnp.where(
            column_at < row_at, straight, jnp.where(column_at > row_at, -turned, 0.0)
        )
        taken = res_c[t, mine, :].astype(jnp.float32)
        real = transposed_product(pick, res_c[t, :, :level])
        imag = transposed_product(pick, res_c[t, :, 2 * level : 3 * level])
        next_real = jnp.where(outer, taken[:, :level], real)
        next_imag = jnp.where(outer, taken[:, 2 * level : 3 * level], -imag)
        inner[t] = jnp.concatenate(
            [
                jnp.where(outer, own_real, next_real),
                jnp.where(outer, next_real, own_real),
                jnp.where(outer, own_imag, next_imag),
                jnp.where(outer, next_imag, own_imag),
            ],
            axis=1,
        ).astype(jnp.bfloat16)

    for point in range(points):
        own_x(point).wait()
        for step in range(1, groups):
            wait_x(point, (me + step) % groups)

    def store(at):
        here = span(at * SUB, SUB)
        return pltpu.make_async_copy(
            result.at[:, :, here, :], out.at[0, :, :, here, :], out_sem.at[at]
        )

    @pl.loop(0, rows // SUB)
    def _(at):
        here = span(at * SUB, SUB)
        value = product(spread[...], got_x[:, :, here, :].reshape(long, states))
        near = inner[:, here, :].reshape(long, states).astype(jnp.float32)
        first = jnp.where(half == 0, near, value)
        second = jnp.where(half == 0, value, near)
        real = jnp.concatenate([first[:, :wide], second[:, :wide]], axis=1)
        imag = jnp.concatenate([first[:, wide:], second[:, wide:]], axis=1)
        result[:, 0, here, :] = real.astype(jnp.bfloat16).reshape(count, SUB, states)
        result[:, 1, here, :] = imag.astype(jnp.bfloat16).reshape(count, SUB, states)
        store(at).start()

    for point in range(points):
        for step in range(1, groups):
            send_x(point, (me + step) % groups).wait_send()
        send_c(point, far, 0, far_near).wait_send()
        send_c(point, half, 1, beside).wait_send()
        send_c(point, half, 2, across).wait_send()
        for source, slot in passing:
            side_c(point, source).wait_send()
            if slot is not None:

                @pl.when(at_entry)
                def _():
                    on_c(point, source, slot).wait_send()

    send_o().wait_send()
    send_d(far, 1 - far, 0, far_near).wait_send()
    send_d(half, low, 1, beside).wait_send()
    send_d(half, 1 - low, 2, across).wait_send()
    for source, slot in passing:
        side_d(source).wait_send()
        if slot is not None:

            @pl.when(at_entry)
            def _():
                on_o(slot, source).wait_send()

    @pl.when(period == 0)
    def _():
        for point in range(points):
            hand(point).wait_send()

    for at in range(rows // SUB):
        store(at).wait()


def fused_body(groups, retarded, scatter_root, coupling, source_index, kernel_weight):
    points = retarded.shape[1]
    states = retarded.shape[3]
    rows = states // groups
    count = points * groups
    dma = pltpu.SemaphoreType.DMA
    kept = jnp.bfloat16
    anywhere = pl.BlockSpec(memory_space=pl.ANY)
    return pl.pallas_call(
        fused,
        out_shape=jax.ShapeDtypeStruct((1, count, 2, rows, states), kept),
        in_specs=[anywhere] * 5,
        out_specs=anywhere,
        scratch_shapes=[
            pltpu.VMEM((points, 2, states, states), kept),
            pltpu.VMEM(scatter_root.shape, jnp.float32),
            pltpu.VMEM((states, states), kept),
            pltpu.VMEM(source_index.shape, jnp.int32),
            pltpu.VMEM(kernel_weight.shape, jnp.float32),
            pltpu.VMEM((2 * states, 2 * states), kept),
            pltpu.VMEM((2 * states, 2 * states), kept),
            pltpu.VMEM((states, 2 * states), kept),
            pltpu.VMEM((states // 2, states), jnp.float32),
            pltpu.VMEM((points, 2, states, states), kept),
            pltpu.VMEM((points, 2, states, states), kept),
            pltpu.VMEM((2, points, rows, states), kept),
            pltpu.VMEM((2, 2, rows, states), kept),
            pltpu.VMEM((groups, points, rows, states), kept),
            pltpu.VMEM((groups, points, rows, states), kept),
            pltpu.VMEM((groups, rows, states), kept),
            pltpu.VMEM((2, rows, states), kept),
            pltpu.VMEM((count, 2 * rows, states), kept),
            pltpu.VMEM((count, 2 * rows, states // 4), kept),
            pltpu.VMEM((count, rows, states), kept),
            pltpu.VMEM((count, 2, rows, states), kept),
            pltpu.VMEM((count * SUB, count * SUB), kept),
            pltpu.VMEM((points, count * SUB, groups * SUB), kept),
            dma((points, 2)),
            dma((4,)),
            dma((points,)),
            dma((points,)),
            dma,
            dma((groups, points)),
            dma((groups, points)),
            dma((3, points)),
            dma((groups, points)),
            dma((2, points)),
            dma((groups, points)),
            dma((3,)),
            dma((groups,)),
            dma((groups,)),
            dma,
            dma((2,)),
            dma((2,)),
            dma((points,)),
            dma((points,)),
            dma((rows // SUB,)),
        ],
        compiler_params=pltpu.CompilerParams(
            collective_id=0, has_side_effects=True, vmem_limit_bytes=LIMIT * 1024 * 1024
        ),
    )(retarded, scatter_root, coupling, source_index, kernel_weight)


def solution(mesh):
    groups = mesh.shape["ek"]

    def chosen(retarded, *others):
        states = retarded.shape[3]
        fits = (
            groups == 8
            and retarded.shape[1] == 2
            and mesh.shape["per"] == 2
            and states % (groups * SUB) == 0
        )
        if fits:
            return fused_body(groups, retarded, *others)
        return body(retarded, *others)

    in_specs = (
        P("per", ("grp", "ek"), None, None, None),
        P("per", ("grp", "ek"), None),
        P(),
        P(),
        P(),
    )
    out_specs = P("per", "grp", None, "ek", None)
    return jax.shard_map(chosen, mesh=mesh, in_specs=in_specs, out_specs=out_specs, check_vma=False)
```

time: 86.9 us -> 81.4 us (0.937)
  Pallas kernels: 81.7 us -> 77.2 us
  local copies, waits for them, and re-layouts: 4.94 us -> 3.91 us
    pallas_call x1, Pallas kernels: 81.7 us -> 77.2 us  [fused_body(): pl.pallas_call(fused, out_shape=jax.ShapeDtypeStruct((1, count, 2, rows,...]
    unnamed x9 -> x1, local copies, waits for them, and re-layouts: 4.94 us -> 3.91 us
where the time goes in v1:
time: 81.4 us; the launch traced here: 81.2 us
  Pallas kernels  77.2 us (95%)
  local copies, waits for them, and re-layouts  3.91 us (5%)
    pallas_call x1, Pallas kernels, fused_body(): pl.pallas_call(fused, out_shape=jax.ShapeDtypeStruct((1, count, 2, rows,...  77.2 us
    unnamed x1, local copies, waits for them, and re-layouts  3.91 us

profile of v1, /device:TPU:1, one launch (start us, length us, event | category | flops | bytes accessed | tf_op | source)
XLA Modules:
  0.0 81.2 jit_solution(11952011823184825783)
XLA Ops:
  0.0 77.2 %shard_map.55 = bf16[1,16,2,80,640]{4,3,2,1,0:T(8,128)(2,1)} custom-call(bf16[1,2,2,640,640]{4,3,2,1,0:T(8,128)(2,1)} %retarded.1, f32[1,2,640]{2,1,0:T(2,128)} %scatter_ref.1, bf16[640,640]{1,0:T(8,128)(2,1)} %coupling_ref.1, s32[16,16]{1,0:T(8,128)} %index_ref.1, f32[16,16]{1,0:T(8,128)} %weight_ref.1), custom_call_target="tpu_custom_call" | custom-call | tf_op jit(solution)/shard_map/pallas_call | solution.py:653
  77.3 3.9 %copy.7 = bf16[1,16,2,80,640]{4,3,2,1,0:T(8,128)(2,1)} copy(bf16[1,16,2,80,640]{4,3,2,1,0:T(8,128)(2,1)} %shard_map.55) | data formatting | bytes 6553600

commit v2 on v1

--- a/solution.py
+++ b/solution.py
@@ -97,7 +97,7 @@
 
 
 SUB = 16
-LIMIT = 58
+LIMIT = 54
 MESH = pl.DeviceIdType.MESH
 
 
@@ -128,7 +128,6 @@
     res_c,
     res_d,
     inner,
-    result,
     spread,
     spread_d,
     load_sem,
@@ -150,7 +149,6 @@
     o_recv,
     hand_sem,
     take_sem,
-    out_sem,
 ):
     groups, points = got_x.shape[:2]
     me = lax.axis_index("ek")
@@ -173,6 +171,7 @@
     far_near = 2 * (2 - half) + side
     far_end = 2 * (3 * far) + side
     at_entry = place == entry
+    turned = (place + period) % 2
 
     def load(point, part):
         return pltpu.make_async_copy(
@@ -204,6 +203,9 @@
     def span(start, size):
         return pl.ds(pl.multiple_of(start, SUB), size)
 
+    def lanes(which):
+        return pl.ds(pl.multiple_of(which * states, states), states)
+
     def remote(source, target, sent, landed, device):
         return pltpu.make_async_remote_copy(
             src_ref=source,
@@ -216,7 +218,7 @@
 
     def send_x(point, device):
         return remote(
-            blocks.at[point, 1 - device // 4, span(device * rows, rows), :],
+            blocks.at[point, span(device * rows, rows), lanes(1 - device // 4)],
             got_x.at[me, point],
             x_send.at[device, point],
             x_recv.at[me, point],
@@ -286,7 +288,9 @@
 
     def own_x(point):
         return pltpu.make_async_copy(
-            blocks.at[point, far, span(me * rows, rows), :], got_x.at[me, point], keep_x.at[point]
+            blocks.at[point, span(me * rows, rows), lanes(far)],
+            got_x.at[me, point],
+            keep_x.at[point],
         )
 
     def own_c(point):
@@ -296,6 +300,45 @@
 
     def own_d():
         return pltpu.make_async_copy(diag.at[half, low], got_d.at[me], keep_d)
+
+    long = count * SUB
+    short = groups * SUB
+
+    def ones(mask):
+        return jnp.where(mask, 1.0, 0.0).astype(jnp.bfloat16)
+
+    def iota(shape, axis):
+        return lax.broadcasted_iota(jnp.int32, shape, axis)
+
+    def fill_spread():
+        small[2].wait()
+        small[3].wait()
+        source_of = index[...]
+        value_of = weight[...]
+        target = lax.broadcasted_iota(jnp.int32, (count, count), 1)
+        matrix = jnp.zeros((count, count), jnp.float32)
+        for tap in range(index.shape[1]):
+            matrix = matrix + jnp.where(
+                source_of[:, tap : tap + 1] == target, value_of[:, tap : tap + 1], 0.0
+            )
+        matrix = matrix.astype(jnp.bfloat16)
+
+        tall = ones(iota((long, count), 0) // SUB == iota((long, count), 1))
+        grown = product(tall, matrix).astype(jnp.bfloat16)
+        spread[...] = jnp.where(
+            iota((long, long), 0) % SUB == iota((long, long), 1) % SUB,
+            transposed_product(grown, tall),
+            0.0,
+        ).astype(jnp.bfloat16)
+        for member in range(points):
+            picked = ones(
+                (iota((short, count), 0) // SUB) * points + member == iota((short, count), 1)
+            )
+            spread_d[member] = jnp.where(
+                iota((long, short), 0) % SUB == iota((long, short), 1) % SUB,
+                transposed_product(grown, picked),
+                0.0,
+            ).astype(jnp.bfloat16)
 
     def fill_stack(point):
         for part in range(2):
@@ -313,56 +356,57 @@
             stack[low_at, states:] = real
 
     def fill_pair(point):
-        @pl.loop(0, 2)
-        def _(band):
-            at = span(band * wide, wide)
-            real = product(green[point, 0, at, :], coupling[...]).astype(jnp.bfloat16)
-            imag = product(green[point, 1, at, :], coupling[...]).astype(jnp.bfloat16)
-            top = span(band * states, wide)
-            low_at = span(band * states + wide, wide)
-            pair[top, :states] = real
-            pair[top, states:] = imag
-            pair[low_at, :states] = -imag
-            pair[low_at, states:] = real
+        real = product(green[point, 0], coupling[...]).astype(jnp.bfloat16)
+        imag = product(green[point, 1], coupling[...]).astype(jnp.bfloat16)
+        for band in range(2):
+            at = slice(band * wide, (band + 1) * wide)
+            top = slice(band * states, band * states + wide)
+            low_at = slice(band * states + wide, (band + 1) * states)
+            pair[top, :states] = real[at, :]
+            pair[top, states:] = imag[at, :]
+            pair[low_at, :states] = -imag[at, :]
+            pair[low_at, states:] = real[at, :]
 
     def fill_moved(point):
         @pl.loop(0, 2)
         def _(band):
             at = span(band * wide, wide)
             top = span(band * states, wide)
+            straight = product(pair[top, :states], before[point])
+            swapped = product(pair[top, states:], before[point])
             for part in range(2):
-                straight = product(pair[top, :states], before[point, part])
-                turned = product(pair[top, states:], before[point, part])
-                real = straight[:, :wide] - turned[:, wide:]
-                imag = straight[:, wide:] + turned[:, :wide]
+                left = slice(part * states, part * states + wide)
+                right = slice(part * states + wide, (part + 1) * states)
+                real = straight[:, left] - swapped[:, right]
+                imag = straight[:, right] + swapped[:, left]
                 moved[at, part * wide : (part + 1) * wide] = real.astype(jnp.bfloat16)
                 moved[at, states + part * wide : states + (part + 1) * wide] = imag.astype(
                     jnp.bfloat16
                 )
 
-    def block(upper, lower):
-        total[...] = transposed_product(
-            stack[span(upper * states, wide), :], stack[span(lower * states, states), :]
-        )
-
-        @pl.when(period == 1)
-        def _():
-            total[...] += transposed_product(
-                moved[span(upper * wide, wide), :], pair[span(lower * states, states), :]
-            )
-
-    row = lax.broadcasted_iota(jnp.int32, (level, level), 0)
-    column = lax.broadcasted_iota(jnp.int32, (level, level), 1)
-    upper_part = row <= column
+    def block(point):
+        @pl.loop(0, 2)
+        def _(band):
+            at = span(band * wide, wide)
+            total[at, :] = transposed_product(stack[span(band * states, wide), :], stack[...])
+
+            @pl.when(period == 1)
+            def _():
+                total[at, :] += transposed_product(moved[at, :], pair[...])
+
+            blocks[point, at, :] = total[at, :].astype(jnp.bfloat16)
+
+    upper_part = lax.broadcasted_iota(jnp.int32, (level, level), 0) <= lax.broadcasted_iota(
+        jnp.int32, (level, level), 1
+    )
 
     def folded(value):
         return [value[:rows, :], value[rows:, :]]
 
     def diagonal(point, which):
-        block(which, which)
-        blocks[point, which, span(which * wide, wide), :] = total[...].astype(jnp.bfloat16)
-        real = total[:level, level : 2 * level]
-        imag = total[:level, 3 * level :]
+        value = total[span(which * wide, wide), lanes(which)]
+        real = value[:level, level : 2 * level]
+        imag = value[:level, 3 * level :]
         cross[which, point] = jnp.concatenate(folded(real) + folded(imag), axis=1).astype(
             jnp.bfloat16
         )
@@ -370,8 +414,8 @@
             at = slice(bit * level, (bit + 1) * level)
             packed = jnp.where(
                 upper_part,
-                total[at, bit * level : (bit + 1) * level],
-                total[at, (2 + bit) * level : (3 + bit) * level],
+                value[at, bit * level : (bit + 1) * level],
+                value[at, (2 + bit) * level : (3 + bit) * level],
             )
             kept = jnp.concatenate(folded(packed), axis=1).astype(jnp.bfloat16)
             for member in range(points):
@@ -380,9 +424,14 @@
                 def _():
                     diag[which, bit, :, member * wide : (member + 1) * wide] = kept
 
-    def crossing(point, which):
-        block(which, 1 - which)
-        blocks[point, 1 - which, span(which * wide, wide), :] = total[...].astype(jnp.bfloat16)
+    def send_far(point):
+        for turn, at_level in enumerate((far, far, half, half)):
+            column = (side + turn + turned) % 2
+            send_x(point, 4 * far + 2 * at_level + column).start()
+
+    def send_near(point):
+        for device in (2 * other + 1 - side, across, beside):
+            send_x(point, device).start()
 
     @pl.loop(0, points)
     def _(point):
@@ -404,19 +453,29 @@
             def _():
                 pl.semaphore_wait(barrier, groups)
 
+            @pl.when(point == 0)
+            def _():
+                fill_spread()
+
             hand(point).wait_recv()
             fill_moved(point)
 
+        block(point)
+
+        @pl.when((period == 0) & (point == 0))
+        def _():
+            pl.semaphore_wait(barrier, groups)
+
+        @pl.when(period == 0)
+        def _():
+            hand(point).start()
+
         @pl.loop(0, 2)
         def _(step):
-            which = jnp.where(step == 0, far, half)
+            which = jnp.where((step == 0) == at_entry, far, half)
             diagonal(point, which)
 
-            @pl.when((period == 0) & (point == 0) & (step == 0))
-            def _():
-                pl.semaphore_wait(barrier, groups)
-
-            @pl.when(step == 0)
+            @pl.when((which == far) & at_entry)
             def _():
                 send_c(point, far, 0, far_near).start()
 
@@ -425,7 +484,7 @@
                     send_o().start()
                     send_d(far, 1 - far, 0, far_near).start()
 
-            @pl.when(step == 1)
+            @pl.when(which == half)
             def _():
                 send_c(point, half, 1, beside).start()
                 send_c(point, half, 2, across).start()
@@ -437,31 +496,39 @@
                     send_d(half, 1 - low, 2, across).start()
                     own_d().start()
 
-            crossing(point, which)
-
-            @pl.when(step == 0)
-            def _():
-                for device in (
-                    4 * far + 2 * far + 1 - side,
-                    4 * far + 2 * half + 1 - side,
-                    4 * far + 2 * far + side,
-                    4 * far + 2 * half + side,
-                ):
-                    send_x(point, device).start()
-
-            @pl.when(step == 1)
-            def _():
-                for device in (2 * other + 1 - side, across, beside):
-                    send_x(point, device).start()
+            @pl.when((which == far) & at_entry & (period == 0))
+            def _():
+                send_far(point)
+
+            @pl.when(which == half)
+            def _():
                 own_x(point).start()
 
-        @pl.when(period == 0)
-        def _():
-            hand(point).start()
+            @pl.when((which == half) & (period == 0))
+            def _():
+                send_near(point)
+
+    @pl.when(~at_entry)
+    def _():
+        for point in range(points):
+            send_c(point, far, 0, far_near).start()
+        send_o().start()
+        send_d(far, 1 - far, 0, far_near).start()
+
+    @pl.when(~at_entry | (period == 1))
+    def _():
+        for point in range(points):
+            send_far(point)
+
+    @pl.when(period == 1)
+    def _():
+        for point in range(points):
+            send_near(point)
 
     @pl.when(period == 0)
     def _():
         small[1].wait()
+        fill_spread()
 
     def pass_c(point, source, slot):
         side_c(point, source).wait_recv()
@@ -485,48 +552,10 @@
         side_d(source).start()
 
     passing = ((far_near, 0), (across, None), (far_end, 1))
-    for point in range(points):
-        for source, slot in passing:
+    for source, slot in passing:
+        for point in range(points):
             pass_c(point, source, slot)
-    for source, slot in passing:
         pass_d(source, slot)
-
-    small[2].wait()
-    small[3].wait()
-    long = count * SUB
-    source_of = index[...]
-    value_of = weight[...]
-    target = lax.broadcasted_iota(jnp.int32, (count, count), 1)
-    matrix = jnp.zeros((count, count), jnp.float32)
-    for tap in range(index.shape[1]):
-        matrix = matrix + jnp.where(
-            source_of[:, tap : tap + 1] == target, value_of[:, tap : tap + 1], 0.0
-        )
-    matrix = matrix.astype(jnp.bfloat16)
-
-    def ones(mask):
-        return jnp.where(mask, 1.0, 0.0).astype(jnp.bfloat16)
-
-    def iota(shape, axis):
-        return lax.broadcasted_iota(jnp.int32, shape, axis)
-
-    tall = ones(iota((long, count), 0) // SUB == iota((long, count), 1))
-    grown = product(tall, matrix).astype(jnp.bfloat16)
-    spread[...] = jnp.where(
-        iota((long, long), 0) % SUB == iota((long, long), 1) % SUB,
-        transposed_product(grown, tall),
-        0.0,
-    ).astype(jnp.bfloat16)
-    short = groups * SUB
-    for member in range(points):
-        picked = ones(
-            (iota((short, count), 0) // SUB) * points + member == iota((short, count), 1)
-        )
-        spread_d[member] = jnp.where(
-            iota((long, short), 0) % SUB == iota((long, short), 1) % SUB,
-            transposed_product(grown, picked),
-            0.0,
-        ).astype(jnp.bfloat16)
 
     own_d().wait()
     for point in range(points):
@@ -537,7 +566,7 @@
             side_c(point, source).wait_recv()
         side_d(source).wait_recv()
 
-    @pl.loop(0, rows // SUB)
+    @pl.loop(0, rows // SUB, unroll=True)
     def _(at):
         here = span(at * SUB, SUB)
         after = span(rows + at * SUB, SUB)
@@ -559,53 +588,54 @@
     pick = ones(row_at == column_at)
     outer = low == 0
 
-    @pl.loop(0, count)
+    @pl.loop(0, count, unroll=8)
     def _(t):
         mine = span(side * rows, rows)
         straight = res_d[t, mine, :].astype(jnp.float32)
-        turned = transposed_product(pick, res_d[t])
-        own_real = jnp.where(column_at >= row_at, straight, turned)
+        mirrored = transposed_product(pick, res_d[t])
+        own_real = jnp.where(column_at >= row_at, straight, mirrored)
         own_imag = jnp.where(
-            column_at < row_at, straight, jnp.where(column_at > row_at, -turned, 0.0)
+            column_at < row_at, straight, jnp.where(column_at > row_at, -mirrored, 0.0)
         )
         taken = res_c[t, mine, :].astype(jnp.float32)
         real = transposed_product(pick, res_c[t, :, :level])
         imag = transposed_product(pick, res_c[t, :, 2 * level : 3 * level])
         next_real = jnp.where(outer, taken[:, :level], real)
         next_imag = jnp.where(outer, taken[:, 2 * level : 3 * level], -imag)
-        inner[t] = jnp.concatenate(
-            [
-                jnp.where(outer, own_real, next_real),
-                jnp.where(outer, next_real, own_real),
-                jnp.where(outer, own_imag, next_imag),
-                jnp.where(outer, next_imag, own_imag),
-            ],
-            axis=1,
+        real = jnp.concatenate(
+            [jnp.where(outer, own_real, next_real), jnp.where(outer, next_real, own_real)], axis=1
         ).astype(jnp.bfloat16)
+        imag = jnp.concatenate(
+            [jnp.where(outer, own_imag, next_imag), jnp.where(outer, next_imag, own_imag)], axis=1
+        ).astype(jnp.bfloat16)
+        inner[t, 0] = real
+        inner[t, 1] = imag
+
+    for which in range(2):
+
+        @pl.when(half == which)
+        def _():
+            out[0, :, :, :, which * wide : (which + 1) * wide] = inner[...]
 
     for point in range(points):
         own_x(point).wait()
         for step in range(1, groups):
             wait_x(point, (me + step) % groups)
 
-    def store(at):
-        here = span(at * SUB, SUB)
-        return pltpu.make_async_copy(
-            result.at[:, :, here, :], out.at[0, :, :, here, :], out_sem.at[at]
-        )
-
-    @pl.loop(0, rows // SUB)
+    @pl.loop(0, rows // SUB, unroll=True)
     def _(at):
         here = span(at * SUB, SUB)
         value = product(spread[...], got_x[:, :, here, :].reshape(long, states))
-        near = inner[:, here, :].reshape(long, states).astype(jnp.float32)
-        first = jnp.where(half == 0, near, value)
-        second = jnp.where(half == 0, value, near)
-        real = jnp.concatenate([first[:, :wide], second[:, :wide]], axis=1)
-        imag = jnp.concatenate([first[:, wide:], second[:, wide:]], axis=1)
-        result[:, 0, here, :] = real.astype(jnp.bfloat16).reshape(count, SUB, states)
-        result[:, 1, here, :] = imag.astype(jnp.bfloat16).reshape(count, SUB, states)
-        store(at).start()
+        real = value[:, :wide].astype(jnp.bfloat16).reshape(count, SUB, wide)
+        imag = value[:, wide:].astype(jnp.bfloat16).reshape(count, SUB, wide)
+        inner[:, 0, here, :] = real
+        inner[:, 1, here, :] = imag
+
+    for which in range(2):
+
+        @pl.when(far == which)
+        def _():
+            out[0, :, :, :, which * wide : (which + 1) * wide] = inner[...]
 
     for point in range(points):
         for step in range(1, groups):
@@ -638,9 +668,6 @@
         for point in range(points):
             hand(point).wait_send()
 
-    for at in range(rows // SUB):
-        store(at).wait()
-
 
 def fused_body(groups, retarded, scatter_root, coupling, source_index, kernel_weight):
     points = retarded.shape[1]
@@ -649,12 +676,12 @@
     count = points * groups
     dma = pltpu.SemaphoreType.DMA
     kept = jnp.bfloat16
-    anywhere = pl.BlockSpec(memory_space=pl.ANY)
+    far_off = pl.BlockSpec(memory_space=pltpu.HBM)
     return pl.pallas_call(
         fused,
-        out_shape=jax.ShapeDtypeStruct((1, count, 2, rows, states), kept),
-        in_specs=[anywhere] * 5,
-        out_specs=anywhere,
+        out_shape=pltpu.VMEM((1, count, 2, rows, states), kept),
+        in_specs=[far_off] * 5,
+        out_specs=pl.BlockSpec(memory_space=pltpu.VMEM),
         scratch_shapes=[
             pltpu.VMEM((points, 2, states, states), kept),
             pltpu.VMEM(scatter_root.shape, jnp.float32),
@@ -664,9 +691,9 @@
             pltpu.VMEM((2 * states, 2 * states), kept),
             pltpu.VMEM((2 * states, 2 * states), kept),
             pltpu.VMEM((states, 2 * states), kept),
-            pltpu.VMEM((states // 2, states), jnp.float32),
-            pltpu.VMEM((points, 2, states, states), kept),
-            pltpu.VMEM((points, 2, states, states), kept),
+            pltpu.VMEM((states, 2 * states), jnp.float32),
+            pltpu.VMEM((points, states, 2 * states), kept),
+            pltpu.VMEM((points, states, 2 * states), kept),
             pltpu.VMEM((2, points, rows, states), kept),
             pltpu.VMEM((2, 2, rows, states), kept),
             pltpu.VMEM((groups, points, rows, states), kept),
@@ -675,8 +702,7 @@
             pltpu.VMEM((2, rows, states), kept),
             pltpu.VMEM((count, 2 * rows, states), kept),
             pltpu.VMEM((count, 2 * rows, states // 4), kept),
-            pltpu.VMEM((count, rows, states), kept),
-            pltpu.VMEM((count, 2, rows, states), kept),
+            pltpu.VMEM((count, 2, rows, states // 2), kept),
             pltpu.VMEM((count * SUB, count * SUB), kept),
             pltpu.VMEM((points, count * SUB, groups * SUB), kept),
             dma((points, 2)),
@@ -698,12 +724,16 @@
             dma((2,)),
             dma((points,)),
             dma((points,)),
-            dma((rows // SUB,)),
         ],
         compiler_params=pltpu.CompilerParams(
             collective_id=0, has_side_effects=True, vmem_limit_bytes=LIMIT * 1024 * 1024
         ),
-    )(retarded, scatter_root, coupling, source_index, kernel_weight)
+    )(
+        *(
+            pltpu.with_memory_space_constraint(array, pltpu.HBM)
+            for array in (retarded, scatter_root, coupling, source_index, kernel_weight)
+        )
+    )
 
 
 def solution(mesh):

time: 81.4 us -> 76.2 us (0.936)
  Pallas kernels: 77.2 us -> 74.3 us
  local copies, waits for them, and re-layouts: 3.91 us -> 1.71 us
    pallas_call x1, Pallas kernels: 77.2 us -> 74.3 us  [fused_body(): pl.pallas_call(fused, out_shape=pltpu.VMEM((1, count, 2, rows, states), k...]
    unnamed x1, local copies, waits for them, and re-layouts: 3.91 us -> 1.71 us
where the time goes in v2:
time: 76.2 us; the launch traced here: 76 us
  Pallas kernels  74.3 us (98%)
  local copies, waits for them, and re-layouts  1.71 us (2%)
    pallas_call x1, Pallas kernels, fused_body(): pl.pallas_call(fused, out_shape=pltpu.VMEM((1, count, 2, rows, states), k...  74.3 us
    unnamed x1, local copies, waits for them, and re-layouts  1.71 us

profile of v2, /device:TPU:1, one launch (start us, length us, event | category | flops | bytes accessed | tf_op | source)
XLA Modules:
  0.0 76.0 jit_solution(715048485756811017)
XLA Ops:
  0.0 74.3 %shard_map.55 = bf16[1,16,2,80,640]{4,3,2,1,0:T(8,128)(2,1)S(1)} custom-call(bf16[1,2,2,640,640]{4,3,2,1,0:T(8,128)(2,1)} %retarded.1, f32[1,2,640]{2,1,0:T(2,128)} %scatter_ref.1, bf16[640,640]{1,0:T(8,128)(2,1)} %coupling_ref.1, s32[16,16]{1,0:T(8,128)} %index_ref.1, f32[16,16]{1,0:T(8,128)} %weight_ref.1), custom_call_target="tpu_custom_call" | custom-call | tf_op jit(solution)/shard_map/pallas_call | solution.py:680
  74.3 1.7 %copy.7 = bf16[1,16,2,80,640]{4,3,2,1,0:T(8,128)(2,1)} copy(bf16[1,16,2,80,640]{4,3,2,1,0:T(8,128)(2,1)S(1)} %shard_map.55) | data formatting | bytes 6553600

commit v3 on v2

--- a/solution.py
+++ b/solution.py
@@ -504,7 +504,7 @@
             def _():
                 own_x(point).start()
 
-            @pl.when((which == half) & (period == 0))
+            @pl.when((which == half) & (period == 1))
             def _():
                 send_near(point)
 
@@ -520,11 +520,6 @@
         for point in range(points):
             send_far(point)
 
-    @pl.when(period == 1)
-    def _():
-        for point in range(points):
-            send_near(point)
-
     @pl.when(period == 0)
     def _():
         small[1].wait()
@@ -556,6 +551,31 @@
         for point in range(points):
             pass_c(point, source, slot)
         pass_d(source, slot)
+
+    @pl.when(period == 0)
+    def _():
+        for point in range(points):
+            send_near(point)
+
+    for point in range(points):
+        own_x(point).wait()
+        for step in range(1, groups):
+            wait_x(point, (me + step) % groups)
+
+    @pl.loop(0, rows // SUB, unroll=True)
+    def _(at):
+        here = span(at * SUB, SUB)
+        value = product(spread[...], got_x[:, :, here, :].reshape(long, states))
+        real = value[:, :wide].astype(jnp.bfloat16).reshape(count, SUB, wide)
+        imag = value[:, wide:].astype(jnp.bfloat16).reshape(count, SUB, wide)
+        inner[:, 0, here, :] = real
+        inner[:, 1, here, :] = imag
+
+    for which in range(2):
+
+        @pl.when(far == which)
+        def _():
+            out[0, :, :, :, which * wide : (which + 1) * wide] = inner[...]
 
     own_d().wait()
     for point in range(points):
@@ -614,26 +634,6 @@
     for which in range(2):
 
         @pl.when(half == which)
-        def _():
-            out[0, :, :, :, which * wide : (which + 1) * wide] = inner[...]
-
-    for point in range(points):
-        own_x(point).wait()
-        for step in range(1, groups):
-            wait_x(point, (me + step) % groups)
-
-    @pl.loop(0, rows // SUB, unroll=True)
-    def _(at):
-        here = span(at * SUB, SUB)
-        value = product(spread[...], got_x[:, :, here, :].reshape(long, states))
-        real = value[:, :wide].astype(jnp.bfloat16).reshape(count, SUB, wide)
-        imag = value[:, wide:].astype(jnp.bfloat16).reshape(count, SUB, wide)
-        inner[:, 0, here, :] = real
-        inner[:, 1, here, :] = imag
-
-    for which in range(2):
-
-        @pl.when(far == which)
         def _():
             out[0, :, :, :, which * wide : (which + 1) * wide] = inner[...]
 

time: 76.2 us -> 72.3 us (0.949)
  Pallas kernels: 74.3 us -> 70.2 us
    pallas_call x1, Pallas kernels: 74.3 us -> 70.2 us  [fused_body(): pl.pallas_call(fused, out_shape=pltpu.VMEM((1, count, 2, rows, states), k...]
where the time goes in v3:
time: 72.3 us; the launch traced here: 72 us
  Pallas kernels  70.2 us (97%)
  local copies, waits for them, and re-layouts  1.71 us (2%)
    pallas_call x1, Pallas kernels, fused_body(): pl.pallas_call(fused, out_shape=pltpu.VMEM((1, count, 2, rows, states), k...  70.2 us
    unnamed x1, local copies, waits for them, and re-layouts  1.71 us

profile of v3, /device:TPU:1, one launch (start us, length us, event | category | flops | bytes accessed | tf_op | source)
XLA Modules:
  0.0 72.0 jit_solution(8794141751757585349)
XLA Ops:
  0.0 70.2 %shard_map.55 = bf16[1,16,2,80,640]{4,3,2,1,0:T(8,128)(2,1)S(1)} custom-call(bf16[1,2,2,640,640]{4,3,2,1,0:T(8,128)(2,1)} %retarded.1, f32[1,2,640]{2,1,0:T(2,128)} %scatter_ref.1, bf16[640,640]{1,0:T(8,128)(2,1)} %coupling_ref.1, s32[16,16]{1,0:T(8,128)} %index_ref.1, f32[16,16]{1,0:T(8,128)} %weight_ref.1), custom_call_target="tpu_custom_call" | custom-call | tf_op jit(solution)/shard_map/pallas_call | solution.py:680
  70.3 1.7 %copy.7 = bf16[1,16,2,80,640]{4,3,2,1,0:T(8,128)(2,1)} copy(bf16[1,16,2,80,640]{4,3,2,1,0:T(8,128)(2,1)S(1)} %shard_map.55) | data formatting | bytes 6553600
